TPU v7x, 128 devices: a whole 4x4x4 slice. The times are simulated.
128 devices in a mesh: xy: 8 (over y, core), gz: 16 (over z, x).
Axes of the slice: x: 4, y: 4, z: 4, core: 2. Of those that a mesh axis runs over, the one named last changes fastest.
Arguments:
- concentration: float32 [256, 64, 4096], P('gz', None, 'xy'), may hold values from -1 to 1
- geometry: float32 [2, 4096], P(None, 'xy'), may hold values from 0.5 to 2
- nbr_elem: int32 [4, 4096], P(None, 'xy'), may hold values from -1 to 4095, as said below
- nbr_edge: int32 [4, 4096], P(None, 'xy'), may hold values from 0 to 7, as said below
- wall_flags: int32 [256], P('gz'), may hold values 0 or 1
Outputs:
- modes: float32 [256, 64, 4096], P('gz', None, 'xy')
Inputs may be any that keep to these rules, and one draw needn't show every extreme that they name: `nbr_elem`: entry [a, e] is the global number of the element across local edge a of element e, or -1 where that edge lies on a wall of the slab; the pairing is mutual. The neighbour is held by the same index of xy or by the index just before or after it, wrapping around; an element with a neighbour on the index before is among the first 64 elements of its device, one with a neighbour on the index after is among the last 64. No element has more than one edge whose neighbour is held by another index of xy. `nbr_edge`: the neighbour's local edge, plus 4 where the two elements number the shared nodes in opposite orders; 0 at walls; the same pairing read from both sides.
All inputs are finite; a program needn't handle non-finite values. No bound on the sum of `wall_flags` on one device may be relied on, other than what follows from the above.
Results may differ from a plain program's by a relative error of at most 0.0001.
Values sent between devices are 32-bit elements; how exact they have to be, the bound alone decides.
A program may use at most 128 MiB of HBM per device.

v0:
```python
import functools

import jax
import jax.numpy as jnp
import ml_dtypes
import numpy as np
from jax import lax
from jax.experimental import pallas as pl
from jax.experimental.pallas import tpu as pltpu
from jax.sharding import PartitionSpec as P

time_step = 0.2
axial_stiffness = 0.002
edge_penalty = 4.0
axial_mobility = 0.002
mobility_floor = 0.05

MESH = pl.DeviceIdType.MESH
f32 = jnp.float32
bf16 = jnp.bfloat16


def point_tables():
    degree = 7
    points = np.arange(degree + 1)
    theta = np.pi * points / degree
    nodes_x = np.cos(theta)
    signs = np.where((points == 0) | (points == degree), 2.0, 1.0) * (-1.0) ** points
    differ = nodes_x[:, None] - nodes_x[None, :]
    deriv = np.outer(signs, 1.0 / signs) / (differ + np.eye(degree + 1))
    deriv = deriv - np.eye(degree + 1) * deriv.sum(axis=1)[:, None]
    inner = np.ones(degree - 1)
    for number in range(1, (degree - 1) // 2 + 1):
        inner = inner - 2.0 * np.cos(2 * number * theta[1:degree]) / (4 * number * number - 1)
    weights = np.zeros(degree + 1)
    weights[1:degree] = 2.0 * inner / degree
    weights[0] = 1.0 / degree**2
    weights[degree] = 1.0 / degree**2
    return (deriv, weights)


def fourier_table(length):
    planes = np.arange(length)
    wave_no = (planes + 1) // 2
    phase = np.outer(wave_no, planes) % length * (2.0 * np.pi / length)
    table = np.where((planes % 2 == 1)[:, None], np.cos(phase), np.sin(phase)) * np.sqrt(
        2.0 / length
    )
    table[0] = 1.0 / np.sqrt(length)
    table[length - 1] = np.cos(phase[length - 1]) / np.sqrt(length)
    return table


def parts(matrix):
    high = matrix.astype(ml_dtypes.bfloat16)
    low = (matrix - high.astype(np.float64)).astype(ml_dtypes.bfloat16)
    return high, low


def four(matrix):
    high, low = parts(matrix)
    return np.concatenate([high, high, low, low], axis=1)


def constants():
    deriv, weights = point_tables()
    grad_x = np.kron(np.eye(8), deriv)
    grad_y = np.kron(deriv, np.eye(8))
    mass = np.kron(weights, weights)
    forward = four(np.concatenate([grad_x, grad_y], axis=0))
    back = np.concatenate([four(grad_x.T * mass), four(grad_y.T * mass)], axis=1)
    stiff_x = grad_x.T @ (mass[:, None] * grad_x)
    stiff_y = grad_y.T @ (mass[:, None] * grad_y)
    stiff = four(np.concatenate([stiff_x, stiff_y], axis=0))
    table = fourier_table(256)
    wave = (np.arange(256) + 1) // 2
    scaled = -axial_mobility * (wave * wave)[:, None] * table
    fh, fl = parts(table)
    gh, gl = parts(scaled)
    fourier = np.concatenate([fh, fh, fl, gh, gh, gl], axis=1)
    mass_b = np.broadcast_to(mass[:, None], (64, 128)).astype(np.float32)
    return forward, back, stiff, fourier, mass_b, [float(w) for w in weights]


def split(value):
    high = value.astype(bf16)
    return high, (value - high.astype(f32)).astype(bf16)


def split4(value):
    high, low = split(value)
    return jnp.concatenate([high, low, high, low], axis=0)


def dot(a, b):
    return jnp.dot(a, b, preferred_element_type=f32)


def lane_groups(shape):
    return lax.broadcasted_iota(jnp.int32, shape, 1) // 32


def swap4(x0, x1, x2, x3):
    group = lane_groups(x0.shape)
    low, even = group < 2, group % 2 == 0
    a0 = jnp.where(low, x0, pltpu.roll(x2, 64, 1))
    a2 = jnp.where(low, pltpu.roll(x0, 64, 1), x2)
    a1 = jnp.where(low, x1, pltpu.roll(x3, 64, 1))
    a3 = jnp.where(low, pltpu.roll(x1, 64, 1), x3)
    return (
        jnp.where(even, a0, pltpu.roll(a1, 32, 1)),
        jnp.where(even, pltpu.roll(a0, 96, 1), a1),
        jnp.where(even, a2, pltpu.roll(a3, 32, 1)),
        jnp.where(even, pltpu.roll(a2, 96, 1), a3),
    )


def node_of(edge, t):
    return (t, 8 * t + 7, 56 + t, 8 * t)[edge]


def kernel(
    edge_w,
    c_ref, geo_ref, nel_ref, ned_ref, flag_ref, fwd_ref, back_ref, stiff_ref, four_ref, mass_ref,
    out_ref,
    cbuf, send1, recv1, ze, zb, send2, recv2, r0, q1, q2, xbuf,
    lane_tab, src_tab, rev_tab, wall_tab, cross_tab, flag_tab, coef_tab, mc_tab,
    hsend, hrecv, dsend, drecv, scal,
    csem, s1sem, r1sem, s2sem, r2sem, hs_sem, hr_sem, ds_sem, dr_sem, osem,
):
    xy = lax.axis_index("xy")
    gz = lax.axis_index("gz")
    z, x = gz // 4, gz % 4

    def load_c(dz):
        tile = (z + dz) % 4
        return pltpu.make_async_copy(
            c_ref.at[:, :, pl.ds(pl.multiple_of(tile * 128, 128), 128)], cbuf.at[dz], csem.at[dz]
        )

    for dz in (1, 3, 0, 2):
        load_c(dz).start()

    barrier = pltpu.get_barrier_semaphore()
    for d in range(1, 16):
        pl.semaphore_signal(barrier, 1, device_id=(xy, (gz + d) % 16), device_id_type=MESH)
    for d in range(1, 8):
        pl.semaphore_signal(barrier, 1, device_id=((xy + d) % 8, gz), device_id_type=MESH)

    scale_x, scale_y = geo_ref[0:1, :], geo_ref[1:2, :]
    jac = 1.0 / (scale_x * scale_y)
    for i, row in enumerate((jac, jac * scale_x * scale_x, jac * scale_y * scale_y)):
        mine = jnp.zeros((8, 128), f32)
        for tile in range(4):
            part = jnp.broadcast_to(row[:, 128 * tile : 128 * tile + 128], (8, 128))
            coef_tab[i, tile] = part
            group = lane_groups((8, 128))
            for d in range(4):
                one = jnp.where(group == d, part, 0.0)
                one = one + pltpu.roll(one, 64, 1)
                one = one + pltpu.roll(one, 32, 1)
                mine = jnp.where((z == tile) & (x == d), one, mine)
        coef_tab[i, 4] = mine
    for a in range(4):
        for tile in range(4):
            cols = slice(128 * tile, 128 * tile + 128)
            elem = jnp.broadcast_to(nel_ref[a : a + 1, cols], (8, 128))
            code = jnp.broadcast_to(ned_ref[a : a + 1, cols], (8, 128))
            wall = elem < 0
            safe = jnp.maximum(elem, 0)
            owner = lax.shift_right_logical(safe, 9)
            local = safe & 511
            lane_tab[a, tile] = local & 127
            src_tab[a, tile] = jnp.where(
                wall, -1, jnp.where(owner == xy, (code & 3) * 4 + lax.shift_right_logical(local, 7), 16)
            )
            rev_tab[a, tile] = jnp.where(code >= 4, 1, 0)
            wall_tab[a, tile] = jnp.where(wall, 1, 0)
            cross_tab[a, tile] = jnp.where((owner != xy) & (elem >= 0), 1, 0)
    mode = lax.broadcasted_iota(jnp.int32, (16, 128), 0)
    flags = jnp.zeros((16, 128), f32)
    for k in range(16):
        flags = jnp.where(mode == k, flag_ref[k].astype(f32), flags)
    flag_tab[...] = flags
    wave = lax.shift_right_logical(mode + 16 * gz + 1, 1).astype(f32)
    mc_tab[...] = 1.0 / time_step + axial_stiffness * wave * wave

    pl.semaphore_wait(barrier, 22)

    def copy1(h, pq):
        return pltpu.make_async_remote_copy(
            send1.at[h, pq], recv1.at[gz, pq], s1sem.at[h], r1sem.at[gz],
            device_id=(xy, h), device_id_type=MESH,
        )

    def pack(s, dz):
        tile = (z + dz) % 4
        pq = s
        ys = swap4(*[cbuf[dz, 4 * pq + pr] for pr in range(4)])
        for d in range(4):
            send1[4 * tile + d, pq] = ys[d]
        for dx in range(4):
            h = 4 * tile + (x + dx) % 4

            @pl.when(h != gz)
            def _():
                copy1(h, pq).start()

    for pair in ((1, 3), (0, 2)):
        for dz in pair:
            load_c(dz).wait()

        def pack_pair(s, carry, pair=pair):
            for dz in pair:
                pack(s, dz)
            return carry

        lax.fori_loop(0, 4, pack_pair, 0)
    recv1[gz] = send1[gz]

    cj, ca, cb = (coef_tab[i, 4][0:1, :] for i in range(3))
    cj4, ca4, cb4 = (jnp.concatenate([v] * 4, axis=1) for v in (cj, ca, cb))
    mass4 = jnp.concatenate([mass_ref[...]] * 4, axis=1)

    def plane_terms(g):
        field = jnp.concatenate([recv1[g, pq] for pq in range(4)], axis=1)
        square = field * field
        chem = square * field - field
        mobility = jnp.maximum(1.0 - square, mobility_floor)
        along = dot(fwd_ref[...], split4(chem))
        flux_x = mobility * along[:64] * ca4
        flux_y = mobility * along[64:] * cb4
        both = jnp.concatenate([split4(flux_x), split4(flux_y)], axis=0)
        weak = dot(back_ref[...], both)
        weight = cj4 * mass4
        explicit = weight * field * (1.0 / time_step) - weak
        bulk = weight * chem
        for value, ref in ((explicit, ze), (bulk, zb)):
            for pq in range(4):
                cols = slice(128 * pq, 128 * pq + 128)
                for jh in range(2):
                    rows = [
                        value[8 * (4 * jh + jl) : 8 * (4 * jh + jl) + 8, cols] for jl in range(4)
                    ]
                    for pr, y in enumerate(swap4(*rows)):
                        start = (g * 16 + 4 * pq + pr) * 16 + 8 * jh
                        ref[pl.ds(pl.multiple_of(start, 8), 8), :] = y

    def from_source(s, carry):
        dz = jnp.where(s < 8, 1 + 2 * (s // 4), 2 * (s // 4 - 2))
        g = ((z + 4 - dz) % 4) * 4 + (x + 4 - s % 4) % 4

        @pl.when(g != gz)
        def _():
            pltpu.make_async_remote_copy(
                send1.at[g], recv1.at[g], s1sem.at[g], r1sem.at[g],
                device_id=(xy, g), device_id_type=MESH,
            ).wait_recv()

        plane_terms(g)
        return carry

    lax.fori_loop(0, 16, from_source, 0)

    def copy2(h, rc):
        rows = pl.ds(rc * 2, 2)
        return pltpu.make_async_remote_copy(
            send2.at[h, rows], recv2.at[gz, rows], s2sem.at[h], r2sem.at[gz],
            device_id=(xy, h), device_id_type=MESH,
        )

    offsets = (1, 4, 3, 12, 10, 5, 15, 7, 13, 2, 8, 6, 9, 14, 11)

    def transform(rc, carry):
        blocks = []
        for ref in (ze, zb):
            pair = [ref[pl.ds(2 * rc + q, 256, stride=16), :] for q in range(2)]
            high, low = split(jnp.concatenate(pair, axis=1))
            blocks += [high, low, high]
        res = dot(four_ref[...], jnp.concatenate(blocks, axis=0))
        for h in range(16):
            for q in range(2):
                send2[h, 2 * rc + q] = res[16 * h : 16 * h + 16, 128 * q : 128 * q + 128]
        for d in offsets:
            copy2((gz + d) % 16, rc).start()
        for q in range(2):
            recv2[gz, 2 * rc + q] = send2[gz, 2 * rc + q]
        return carry

    lax.fori_loop(0, 8, transform, 0)

    def settle2(d, carry):
        g = (gz + d) % 16
        pltpu.make_async_remote_copy(
            send2.at[g], recv2.at[g], s2sem.at[g], r2sem.at[g],
            device_id=(xy, g), device_id_type=MESH,
        ).wait_recv()
        return carry

    lax.fori_loop(1, 16, settle2, 0)

    recv2f = recv2.reshape(16 * 16 * 16, 128)

    def assemble(k, tile):
        for jh in range(2):
            xs = [
                recv2f[pl.ds(((4 * tile + s) * 16 + 8 * jh) * 16 + k, 8, stride=16), :]
                for s in range(4)
            ]
            for jl, y in enumerate(swap4(*xs)):
                start = (tile * 16 + k) * 64 + (4 * jh + jl) * 8
                r0[pl.ds(pl.multiple_of(start, 8), 8), :] = y

    def interior(src, dst, tile, kq):
        rows = [pl.ds(pl.multiple_of((tile * 16 + 4 * kq + s) * 64, 64), 64) for s in range(4)]
        field = jnp.concatenate([src[r, :] for r in rows], axis=1)
        res = dot(stiff_ref[...], split4(field))
        cj_t, ca_t, cb_t = (coef_tab[i, tile][0:1, :] for i in range(3))
        weight = mass_ref[...] * cj_t
        for s in range(4):
            cols = slice(128 * s, 128 * s + 128)
            mc = mc_tab[pl.ds(4 * kq + s, 1), :]
            dst[rows[s], :] = (
                weight * mc * field[:, cols] + ca_t * res[:64, cols] + cb_t * res[64:, cols]
            )

    def first_pass(s, carry):
        tile, kq = s // 4, s % 4
        for k in range(4):
            assemble(4 * kq + k, tile)
        interior(r0, q1, tile, kq)
        return carry

    lax.fori_loop(0, 16, first_pass, 0)

    def second_pass(s, carry):
        interior(q1, q2, s // 4, s % 4)
        return carry

    def trace(ref, tile, edge, t):
        return ref[pl.ds(tile * 1024 + node_of(edge, t), 16, stride=64), :]

    def halo_copy(which, side):
        peer = (xy + (7, 1)[side]) % 8
        return pltpu.make_async_remote_copy(
            hsend.at[which, side], hrecv.at[which, side],
            hs_sem.at[which, side], hr_sem.at[which, side],
            device_id=(peer, gz), device_id_type=MESH,
        )

    def send_halo(ref, which):
        for side, tile in ((0, 0), (1, 3)):

            def fill(t, carry, side=side, tile=tile):
                value = jnp.zeros((16, 128), f32)
                for a in range(4):
                    on = jnp.concatenate([cross_tab[a, tile]] * 2, axis=0) > 0
                    value = jnp.where(on, trace(ref, tile, a, t), value)
                hsend[which, side, t] = value
                return carry

            lax.fori_loop(0, 8, fill, 0)
            halo_copy(which, side).start()

    def penalize(src, dst, which):
        for side in range(2):
            halo_copy(which, side).wait_recv()
        first = lax.broadcasted_iota(jnp.int32, (16, 128), 1) < 64
        flag = flag_tab[...]

        def one(s, carry):
            tp, tile = s // 4, s % 4
            ts = (tp, 7 - tp)
            weight = jnp.where(
                tp == 0, edge_w[0], jnp.where(tp == 1, edge_w[1], jnp.where(tp == 2, edge_w[2], edge_w[3]))
            ) * edge_penalty
            for a in range(4):
                two = lambda tab: jnp.concatenate([tab[a, tile]] * 2, axis=0)
                lane, source, rev, wall = (two(t) for t in (lane_tab, src_tab, rev_tab, wall_tab))
                rev, wall = rev > 0, wall > 0
                got = [jnp.zeros((16, 128), f32) for _ in ts]
                for b in range(4):
                    for tile_b in range(4):
                        here = source == 4 * b + tile_b
                        for i, t in enumerate(ts):
                            picked = jnp.take_along_axis(trace(src, tile_b, b, t), lane, axis=1)
                            got[i] = jnp.where(here, picked, got[i])
                here = source == 16
                for i, t in enumerate(ts):
                    side = jnp.where(first, hrecv[which, 0, t], hrecv[which, 1, t])
                    picked = jnp.take_along_axis(side, lane, axis=1)
                    got[i] = jnp.where(here, picked, got[i])
                other = [jnp.where(rev, got[1 - i], got[i]) for i in range(2)]
                factor = jnp.where(wall, flag, 1.0)
                for i, t in enumerate(ts):
                    pen = weight * (factor * trace(src, tile, a, t) - other[i])
                    at = pl.ds(tile * 1024 + node_of(a, t), 16, stride=64)
                    dst[at, :] = dst[at, :] + pen
            return carry

        lax.fori_loop(0, 16, one, 0)

    def total(which, n):
        for d in range(1, 8):
            pltpu.make_async_remote_copy(
                dsend.at[which], drecv.at[which, xy], ds_sem.at[which, (xy + d) % 8],
                dr_sem.at[which, xy], device_id=((xy + d) % 8, gz), device_id_type=MESH,
            ).start()
        drecv[which, xy] = dsend[which]

    def total_done(which, n):
        for d in range(1, 8):
            g = (xy + d) % 8
            pltpu.make_async_remote_copy(
                dsend.at[which], drecv.at[which, g], ds_sem.at[which, g],
                dr_sem.at[which, g], device_id=(g, gz), device_id_type=MESH,
            ).wait_recv()
        out = []
        for i in range(n):
            acc = drecv[which, 0, i]
            for g in range(1, 8):
                acc = acc + drecv[which, g, i]
            out.append(jnp.broadcast_to(jnp.sum(acc, axis=1, keepdims=True), (16, 128)))
        return out

    def rows_of(tile, k):
        return pl.ds(pl.multiple_of((tile * 16 + k) * 64, 64), 64)

    def sum8(value):
        return jnp.sum(value, axis=0, keepdims=True)

    send_halo(r0, 0)
    penalize(r0, q1, 0)
    send_halo(q1, 1)

    def dots1(k, carry):
        rr = jnp.zeros((64, 128), f32)
        pq = jnp.zeros((64, 128), f32)
        for tile in range(4):
            a, b = r0[rows_of(tile, k), :], q1[rows_of(tile, k), :]
            rr, pq = rr + a * a, pq + a * b
        dsend[0, 0, pl.ds(k, 1), :] = sum8(rr)
        dsend[0, 1, pl.ds(k, 1), :] = sum8(pq)
        return carry

    lax.fori_loop(0, 16, dots1, 0)
    total(0, 2)
    lax.fori_loop(0, 16, second_pass, 0)
    penalize(q1, q2, 1)
    rr0, pq0 = total_done(0, 2)
    scal[0] = rr0 / pq0

    def dots2(k, carry):
        accs = [jnp.zeros((64, 128), f32) for _ in range(3)]
        alpha = scal[0, pl.ds(k, 1), :]
        for tile in range(4):
            rows = rows_of(tile, k)
            u, v = r0[rows, :], q1[rows, :]
            r1 = u - alpha * v
            s = v - alpha * q2[rows, :]
            for i, term in enumerate((r1 * r1, r1 * s, r1 * v + u * s)):
                accs[i] = accs[i] + term
        for i in range(3):
            dsend[1, i, pl.ds(k, 1), :] = sum8(accs[i])
        return carry

    lax.fori_loop(0, 16, dots2, 0)
    total(1, 3)
    rr1, r1s, cross = total_done(1, 3)
    alpha0 = rr0 / pq0
    beta = rr1 / rr0
    alpha1 = rr1 / (r1s + beta * cross + beta * beta * pq0)
    scal[1] = alpha0 + alpha1 * (1.0 + beta)
    scal[2] = alpha1 * alpha0

    def finish(tile, carry):
        def one(k, carry):
            rows = rows_of(tile, k)
            xbuf[tile, k] = (
                scal[1, pl.ds(k, 1), :] * r0[rows, :] - scal[2, pl.ds(k, 1), :] * q1[rows, :]
            )
            return carry

        lax.fori_loop(0, 16, one, 0)
        out_copy(tile).start()
        return carry

    def out_copy(tile):
        return pltpu.make_async_copy(
            xbuf.at[tile],
            out_ref.at[:, :, pl.ds(pl.multiple_of(tile * 128, 128), 128)],
            osem.at[tile],
        )

    lax.fori_loop(0, 4, finish, 0)

    def sent(d, carry):
        g = (gz + d) % 16
        for buf, dst, ssem, rsem in ((send1, recv1, s1sem, r1sem), (send2, recv2, s2sem, r2sem)):
            pltpu.make_async_remote_copy(
                buf.at[g], dst.at[g], ssem.at[g], rsem.at[g], device_id=(xy, g), device_id_type=MESH
            ).wait_send()
        return carry

    lax.fori_loop(1, 16, sent, 0)
    for which in range(2):
        for side in range(2):
            halo_copy(which, side).wait_send()
        for d in range(1, 8):
            g = (xy + d) % 8
            pltpu.make_async_remote_copy(
                dsend.at[which], drecv.at[which, g], ds_sem.at[which, g],
                dr_sem.at[which, g], device_id=(g, gz), device_id_type=MESH,
            ).wait_send()
    for tile in range(4):
        out_copy(tile).wait()


def per_device(concentration, geometry, nbr_elem, nbr_edge, wall_flags):
    forward, back, stiff, fourier, mass_b, edge_w = constants()
    vmem = pl.BlockSpec(memory_space=pltpu.VMEM)
    dma = pltpu.SemaphoreType.DMA
    V = pltpu.VMEM
    i32 = jnp.int32
    return pl.pallas_call(
        functools.partial(kernel, edge_w),
        out_shape=jax.ShapeDtypeStruct(concentration.shape, f32),
        in_specs=[pl.BlockSpec(memory_space=pl.ANY), vmem, vmem, vmem, pl.BlockSpec(memory_space=pltpu.SMEM)]
        + [vmem] * 5,
        out_specs=pl.BlockSpec(memory_space=pl.ANY),
        scratch_shapes=[
            V((4, 16, 64, 128), f32),
            V((16, 4, 64, 128), f32),
            V((16, 4, 64, 128), f32),
            V((4096, 128), f32),
            V((4096, 128), f32),
            V((16, 16, 16, 128), f32),
            V((16, 16, 16, 128), f32),
            V((4096, 128), f32),
            V((4096, 128), f32),
            V((4096, 128), f32),
            V((4, 16, 64, 128), f32),
            V((4, 4, 8, 128), i32),
            V((4, 4, 8, 128), i32),
            V((4, 4, 8, 128), i32),
            V((4, 4, 8, 128), i32),
            V((4, 4, 8, 128), i32),
            V((16, 128), f32),
            V((3, 5, 8, 128), f32),
            V((16, 128), f32),
            V((2, 2, 8, 16, 128), f32),
            V((2, 2, 8, 16, 128), f32),
            V((2, 3, 16, 128), f32),
            V((2, 8, 3, 16, 128), f32),
            V((3, 16, 128), f32),
            dma((4,)),
            dma((16,)),
            dma((16,)),
            dma((16,)),
            dma((16,)),
            dma((2, 2)),
            dma((2, 2)),
            dma((2, 8)),
            dma((2, 8)),
            dma((4,)),
        ],
        compiler_params=pltpu.CompilerParams(
            collective_id=0, has_side_effects=True, vmem_limit_bytes=50 << 20
        ),
    )(
        concentration, geometry, nbr_elem, nbr_edge, wall_flags,
        jnp.asarray(forward), jnp.asarray(back), jnp.asarray(stiff), jnp.asarray(fourier),
        jnp.asarray(mass_b),
    )


def solution(mesh):
    return jax.shard_map(
        per_device,
        mesh=mesh,
        in_specs=(P("gz", None, "xy"), P(None, "xy"), P(None, "xy"), P(None, "xy"), P("gz")),
        out_specs=P("gz", None, "xy"),
        check_vma=False,
    )
```

profile of v0, /device:TPU:1, one launch (start us, length us, event | category | flops | bytes accessed | tf_op | source)
XLA Modules:
  0.0 127.3 jit_solution(4767976739424636236)
XLA Ops:
  0.0 0.0 copy-start
  0.0 1.1 copy-done
  1.1 0.0 copy-start.1
  1.1 0.8 copy-done.1
  2.0 0.0 copy-start.2
  2.0 0.8 copy-done.2
  2.8 0.0 copy-start.3
  2.8 0.8 copy-done.3
  3.7 0.0 copy-start.4
  3.7 0.8 copy-done.4
  4.4 0.0 copy-start.5
  4.4 0.7 copy-done.5
  5.1 0.0 copy-start.6
  5.1 0.7 copy-done.6
  5.8 0.0 copy-start.7
  5.8 0.7 copy-done.7
  6.5 0.0 copy-start.8
  6.5 0.7 copy-done.8
  7.2 118.8 %shard_map.100 = f32[16,64,512]{2,1,0:T(8,128)S(1)} custom-call(f32[16,64,512]{2,1,0:T(8,128)} %c_ref.1, f32[2,512]{1,0:T(2,128)S(1)} %copy-done.7, s32[4,512]{1,0:T(4,128)S(1)} %copy-done.5, s32[4,512]{1,0:T(4,128)S(1)} %copy-done.6, s32[16]{0:T(128)S(1)} %copy-done.8, bf16[128,256]{1,0:T(8,128)(2,1)S(1)} %copy-done.3, bf16[64,512]{1,0:T(8,128)(2,1)S(1)} %copy-done.2, ...), custom_call_target="tpu_custom_call" | custom-call | tf_op jit(solution)/shard_map/pallas_call | solution.py:525
  126.0 1.3 %copy.12 = f32[16,64,512]{2,1,0:T(8,128)} copy(f32[16,64,512]{2,1,0:T(8,128)S(1)} %shard_map.100) | data formatting | bytes 4194304
Async XLA Ops:
  0.0 1.1 copy-start
  1.1 0.8 copy-start.1
  2.0 0.8 copy-start.2
  2.8 0.8 copy-start.3
  3.7 0.8 copy-start.4
  4.4 0.7 copy-start.5
  5.1 0.7 copy-start.6
  5.8 0.7 copy-start.7
  6.5 0.7 copy-start.8
where the time goes:
time: 128 us; the launch traced here: 127 us
  Pallas kernels  119 us (93%)
  local copies, waits for them, and re-layouts  8.46 us (7%)
    pallas_call x1, Pallas kernels, per_device(): pl.pallas_call(functools.partial(kernel, edge_w), out_shape=jax.ShapeDtyp...  119 us
    unnamed x19, local copies, waits for them, and re-layouts  8.46 us

commit v1 on v0

v1 whole, which is shorter than its diff:
```python
import functools

import jax
import jax.numpy as jnp
import ml_dtypes
import numpy as np
from jax import lax
from jax.experimental import pallas as pl
from jax.experimental.pallas import tpu as pltpu
from jax.sharding import PartitionSpec as P

time_step = 0.2
axial_stiffness = 0.002
edge_penalty = 4.0
axial_mobility = 0.002
mobility_floor = 0.05

MESH = pl.DeviceIdType.MESH
f32 = jnp.float32
bf16 = jnp.bfloat16


def point_tables():
    degree = 7
    points = np.arange(degree + 1)
    theta = np.pi * points / degree
    nodes_x = np.cos(theta)
    signs = np.where((points == 0) | (points == degree), 2.0, 1.0) * (-1.0) ** points
    differ = nodes_x[:, None] - nodes_x[None, :]
    deriv = np.outer(signs, 1.0 / signs) / (differ + np.eye(degree + 1))
    deriv = deriv - np.eye(degree + 1) * deriv.sum(axis=1)[:, None]
    inner = np.ones(degree - 1)
    for number in range(1, (degree - 1) // 2 + 1):
        inner = inner - 2.0 * np.cos(2 * number * theta[1:degree]) / (4 * number * number - 1)
    weights = np.zeros(degree + 1)
    weights[1:degree] = 2.0 * inner / degree
    weights[0] = 1.0 / degree**2
    weights[degree] = 1.0 / degree**2
    return (deriv, weights)


def fourier_table(length):
    planes = np.arange(length)
    wave_no = (planes + 1) // 2
    phase = np.outer(wave_no, planes) % length * (2.0 * np.pi / length)
    table = np.where((planes % 2 == 1)[:, None], np.cos(phase), np.sin(phase)) * np.sqrt(
        2.0 / length
    )
    table[0] = 1.0 / np.sqrt(length)
    table[length - 1] = np.cos(phase[length - 1]) / np.sqrt(length)
    return table


def parts(matrix):
    high = matrix.astype(ml_dtypes.bfloat16)
    low = (matrix - high.astype(np.float64)).astype(ml_dtypes.bfloat16)
    return high, low


def four(matrix):
    high, low = parts(matrix)
    return np.concatenate([high, high, low, low], axis=1)


def constants():
    deriv, weights = point_tables()
    grad_x = np.kron(np.eye(8), deriv)
    grad_y = np.kron(deriv, np.eye(8))
    mass = np.kron(weights, weights)
    forward = four(np.concatenate([grad_x, grad_y], axis=0))
    back = np.concatenate([four(grad_x.T * mass), four(grad_y.T * mass)], axis=1)
    table = fourier_table(256)
    wave = (np.arange(256) + 1) // 2
    scaled = -axial_mobility * (wave * wave)[:, None] * table
    fh, fl = parts(table)
    gh, gl = parts(scaled)
    fourier = np.concatenate([fh, fh, fl, gh, gh, gl], axis=1)
    mass_b = np.broadcast_to(mass[:, None], (64, 128)).astype(np.float32)
    line = deriv.T @ (weights[:, None] * deriv)
    return forward, back, fourier, mass_b, weights, line


def split(value):
    high = value.astype(bf16)
    return high, (value - high.astype(f32)).astype(bf16)


def split4(value):
    high, low = split(value)
    return jnp.concatenate([high, low, high, low], axis=0)


def dot(a, b):
    return jnp.dot(a, b, preferred_element_type=f32)


def lane_groups(shape):
    return lax.broadcasted_iota(jnp.int32, shape, 1) // 32


def swap4(x0, x1, x2, x3):
    group = lane_groups(x0.shape)
    low, even = group < 2, group % 2 == 0
    a0 = jnp.where(low, x0, pltpu.roll(x2, 64, 1))
    a2 = jnp.where(low, pltpu.roll(x0, 64, 1), x2)
    a1 = jnp.where(low, x1, pltpu.roll(x3, 64, 1))
    a3 = jnp.where(low, pltpu.roll(x1, 64, 1), x3)
    return (
        jnp.where(even, a0, pltpu.roll(a1, 32, 1)),
        jnp.where(even, pltpu.roll(a0, 96, 1), a1),
        jnp.where(even, a2, pltpu.roll(a3, 32, 1)),
        jnp.where(even, pltpu.roll(a2, 96, 1), a3),
    )


def node_of(edge, t):
    return (t, 8 * t + 7, 56 + t, 8 * t)[edge]


def apply_line(line, us):
    even = [us[m] + us[7 - m] for m in range(4)]
    odd = [us[m] - us[7 - m] for m in range(4)]
    out = [None] * 8
    for i in range(4):
        e = o = None
        for m in range(4):
            ce = float(0.5 * (line[i, m] + line[i, 7 - m]))
            co = float(0.5 * (line[i, m] - line[i, 7 - m]))
            e = ce * even[m] if e is None else e + ce * even[m]
            o = co * odd[m] if o is None else o + co * odd[m]
        out[i], out[7 - i] = e + o, e - o
    return out


def kernel(
    weights, line,
    c_ref, geo_hbm, nel_hbm, ned_hbm, flag_hbm, fwd_hbm, back_hbm, four_hbm, mass_hbm,
    out_ref,
    geo_ref, nel_ref, ned_ref, flag_ref, fwd_ref, back_ref, four_ref, mass_ref,
    cbuf, send1, recv1, ze, zb, send2, recv2, r0, q1, q2, rt, qt,
    lane_tab, src_tab, rev_tab, wall_tab, cross_tab, flag_tab, coef_tab, mc_tab,
    hsend, hrecv, dsend, drecv,
    csem, isem, s1sem, r1sem, s2sem, r2sem, hs_sem, hr_sem, ds_sem, dr_sem,
):
    xy = lax.axis_index("xy")
    gz = lax.axis_index("gz")
    z, x = gz // 4, gz % 4
    PHASES = ((1, 1), (1, 0), (0, 1), (0, 0))

    def tile_of(phase):
        return 2 * ((z + phase[0]) % 2) + (x + phase[1]) % 2

    def device_at(tile, d):
        return 4 * (2 * (d // 2) + tile // 2) + 2 * (d % 2) + tile % 2

    def d_of(j):
        return 2 * ((z // 2 + j // 2) % 2) + (x // 2 + j) % 2

    def load_c(i):
        tile = tile_of(PHASES[i])
        return pltpu.make_async_copy(
            c_ref.at[:, :, pl.ds(pl.multiple_of(tile * 128, 128), 128)], cbuf.at[i], csem.at[i]
        )

    for i in range(4):
        load_c(i).start()

    barrier = pltpu.get_barrier_semaphore()
    for d in range(1, 16):
        pl.semaphore_signal(barrier, 1, device_id=(xy, (gz + d) % 16), device_id_type=MESH)
    for d in range(1, 8):
        pl.semaphore_signal(barrier, 1, device_id=((xy + d) % 8, gz), device_id_type=MESH)

    loads = [
        pltpu.make_async_copy(src, dst, isem.at[i])
        for i, (src, dst) in enumerate(
            (
                (geo_hbm, geo_ref), (nel_hbm, nel_ref), (ned_hbm, ned_ref), (flag_hbm, flag_ref),
                (fwd_hbm, fwd_ref), (back_hbm, back_ref), (mass_hbm, mass_ref), (four_hbm, four_ref),
            )
        )
    ]
    for load in loads:
        load.start()

    for i in range(4):
        load_c(i).wait()

        def pack(pq, carry, i=i):
            tile = tile_of(PHASES[i])
            ys = swap4(*[cbuf[i, 4 * pq + pr] for pr in range(4)])
            for d in range(4):
                send1[device_at(tile, d), pq] = ys[d]
            return carry

        lax.fori_loop(0, 4, pack, 0)
    recv1[gz] = send1[gz]

    for load in loads:
        load.wait()
    scale_x, scale_y = geo_ref[0:1, :], geo_ref[1:2, :]
    jac = 1.0 / (scale_x * scale_y)
    my_tile, my_d = tile_of((0, 0)), d_of(0)
    for i, row in enumerate((jac, jac * scale_x * scale_x, jac * scale_y * scale_y)):
        mine = jnp.zeros((8, 128), f32)
        for tile in range(4):
            part = jnp.broadcast_to(row[:, 128 * tile : 128 * tile + 128], (8, 128))
            coef_tab[i, tile] = part
            group = lane_groups((8, 128))
            for d in range(4):
                one = jnp.where(group == d, part, 0.0)
                one = one + pltpu.roll(one, 64, 1)
                one = one + pltpu.roll(one, 32, 1)
                mine = jnp.where((my_tile == tile) & (my_d == d), one, mine)
        coef_tab[i, 4] = mine
    for a in range(4):
        for tile in range(4):
            cols = slice(128 * tile, 128 * tile + 128)
            elem = jnp.broadcast_to(nel_ref[a : a + 1, cols], (8, 128))
            code = jnp.broadcast_to(ned_ref[a : a + 1, cols], (8, 128))
            wall = elem < 0
            safe = jnp.maximum(elem, 0)
            owner = lax.shift_right_logical(safe, 9)
            local = safe & 511
            lane_tab[a, tile] = local & 127
            src_tab[a, tile] = jnp.where(
                wall, -1, jnp.where(owner == xy, (code & 3) * 4 + lax.shift_right_logical(local, 7), 16)
            )
            rev_tab[a, tile] = jnp.where(code >= 4, 1, 0)
            wall_tab[a, tile] = jnp.where(wall, 1, 0)
            cross_tab[a, tile] = jnp.where((owner != xy) & (elem >= 0), 1, 0)
    sub = lax.broadcasted_iota(jnp.int32, (8, 128), 0)
    for kh in range(2):
        flags = jnp.zeros((8, 128), f32)
        for k in range(8):
            flags = jnp.where(sub == k, flag_ref[8 * kh + k].astype(f32), flags)
        flag_tab[kh] = flags
        wave = lax.shift_right_logical(sub + 8 * kh + 16 * gz + 1, 1).astype(f32)
        mc_tab[kh] = 1.0 / time_step + axial_stiffness * wave * wave

    def source(s):
        a, b = 1 - s // 8, 1 - (s // 4) % 2
        return device_at(2 * ((z + a) % 2) + (x + b) % 2, d_of(s % 4))

    pl.semaphore_wait(barrier, 22)

    def copy1(h, pq):
        return pltpu.make_async_remote_copy(
            send1.at[h, pq], recv1.at[gz, pq], s1sem.at[h], r1sem.at[gz],
            device_id=(xy, h), device_id_type=MESH,
        )

    def block1(g):
        return pltpu.make_async_remote_copy(
            send1.at[g], recv1.at[g], s1sem.at[g], r1sem.at[g],
            device_id=(xy, g), device_id_type=MESH,
        )

    def others(i, act):
        def one(j, carry):
            h = source(4 * i + j)

            @pl.when(h != gz)
            def _():
                act(h)

            return carry

        lax.fori_loop(0, 4, one, 0)

    def issue1(i):
        for pq in range(4):
            others(i, lambda h, pq=pq: copy1(h, pq).start())

    issue1(0)
    issue1(1)

    cj, ca, cb = (coef_tab[i, 4][0:1, :] for i in range(3))
    cj4, ca4, cb4 = (jnp.concatenate([v] * 4, axis=1) for v in (cj, ca, cb))
    mass4 = jnp.concatenate([mass_ref[...]] * 4, axis=1)

    def plane_terms(g):
        field = jnp.concatenate([recv1[g, pq] for pq in range(4)], axis=1)
        square = field * field
        chem = square * field - field
        mobility = jnp.maximum(1.0 - square, mobility_floor)
        along = dot(fwd_ref[...], split4(chem))
        flux_x = mobility * along[:64] * ca4
        flux_y = mobility * along[64:] * cb4
        both = jnp.concatenate([split4(flux_x), split4(flux_y)], axis=0)
        weak = dot(back_ref[...], both)
        weight = cj4 * mass4
        explicit = weight * field * (1.0 / time_step) - weak
        bulk = weight * chem
        for value, ref in ((explicit, ze), (bulk, zb)):
            for pq in range(4):
                cols = slice(128 * pq, 128 * pq + 128)
                for jh in range(2):
                    rows = [
                        value[8 * (4 * jh + jl) : 8 * (4 * jh + jl) + 8, cols] for jl in range(4)
                    ]
                    for pr, y in enumerate(swap4(*rows)):
                        start = (g * 16 + 4 * pq + pr) * 16 + 8 * jh
                        ref[pl.ds(pl.multiple_of(start, 8), 8), :] = y

    plane_terms(gz)

    def phase1(i, carry):
        others(i, lambda h: block1(h).wait_send())

        @pl.when(i < 2)
        def _():
            issue1(i + 2)

        def take(g):
            block1(g).wait_recv()
            plane_terms(g)

        others(i, take)
        return carry

    lax.fori_loop(0, 4, phase1, 0)

    def copy2(h, kh, which, start, size):
        rows = pl.ds(start, size)
        return pltpu.make_async_remote_copy(
            send2.at[h, kh, rows], recv2.at[gz, kh, rows], s2sem.at[h, which], r2sem.at[gz, kh],
            device_id=(xy, h), device_id_type=MESH,
        )

    def transform(rc, carry):
        blocks = []
        for ref in (ze, zb):
            pair = [ref[pl.ds(2 * rc + q, 256, stride=16), :] for q in range(2)]
            high, low = split(jnp.concatenate(pair, axis=1))
            blocks += [high, low, high]
        res = dot(four_ref[...], jnp.concatenate(blocks, axis=0))
        for h in range(16):
            for kh in range(2):
                for q in range(2):
                    row = 16 * h + 8 * kh
                    send2[h, kh, 2 * rc + q] = res[row : row + 8, 128 * q : 128 * q + 128]
        which = rc // 6
        for i in range(4):
            for j in range(4):
                if PHASES[i] == (0, 0) and j == 0:
                    continue
                copy2(device_at(tile_of(PHASES[i]), d_of(j)), 0, which, 2 * rc, 2).start()
        return carry

    lax.fori_loop(0, 8, transform, 0)
    recv2[gz] = send2[gz]

    DEPTH = 3

    def portion(p, act):
        others(p // 4, lambda h: act(copy2(h, 1, 2 + p % 4, 4 * (p % 4), 4)))

    def pump(p):
        pass

    def early(i, carry):
        others(i, lambda h: copy2(h, 0, 0, 0, 12).wait_send())
        return carry

    lax.fori_loop(0, 4, early, 0)
    for p in range(8):
        portion(p, lambda copy: copy.start())

    def arrived(kh, i):
        others(
            i,
            lambda g: pltpu.make_async_remote_copy(
                send2.at[g, kh], recv2.at[g, kh], s2sem.at[g, kh], r2sem.at[g, kh],
                device_id=(xy, g), device_id_type=MESH,
            ).wait_recv(),
        )

    def assemble(kh, tile):
        devices = [device_at(tile, d) for d in range(4)]
        for r in range(16):
            xs = [recv2[g, kh, r] for g in devices]
            for jl, y in enumerate(swap4(*xs)):
                r0[kh, tile, 32 * (r // 8) + 8 * jl + r % 8] = y

    def interior(src, dst, kh, tile):
        cj_t, ca_t, cb_t = (coef_tab[i, tile] for i in range(3))
        cjm = cj_t * mc_tab[kh]
        for j in range(8):
            us = [src[kh, tile, 8 * j + i] for i in range(8)]
            cjw, caw = cjm * float(weights[j]), ca_t * float(weights[j])
            for i, value in enumerate(apply_line(line, us)):
                dst[kh, tile, 8 * j + i] = caw * value + (cjw * float(weights[i])) * us[i]
        for i in range(8):
            us = [src[kh, tile, 8 * j + i] for j in range(8)]
            cbw = cb_t * float(weights[i])
            for j, value in enumerate(apply_line(line, us)):
                dst[kh, tile, 8 * j + i] = dst[kh, tile, 8 * j + i] + cbw * value

    def first_pass(kh):
        def one(i, carry):
            arrived(kh, i)
            if kh == 0:

                @pl.when(i % 2 == 1)
                def _():
                    pump(3 + i // 2)

            tile = 2 * ((z + 1 - i // 2) % 2) + (x + 1 - i % 2) % 2
            assemble(kh, tile)
            interior(r0, q1, kh, tile)
            return carry

        lax.fori_loop(0, 4, one, 0)

    def second_pass(kh):
        def one(tile, carry):
            interior(q1, q2, kh, tile)
            return carry

        lax.fori_loop(0, 4, one, 0)

    def halo_copy(which, side):
        peer = (xy + (7, 1)[side]) % 8
        return pltpu.make_async_remote_copy(
            hsend.at[which, side], hrecv.at[which, side],
            hs_sem.at[which, side], hr_sem.at[which, side],
            device_id=(peer, gz), device_id_type=MESH,
        )

    def send_halo(ref, kh, which):
        for side, tile in ((0, 0), (1, 3)):
            on = [cross_tab[a, tile] > 0 for a in range(4)]
            for t in range(8):
                value = jnp.zeros((8, 128), f32)
                for a in range(4):
                    value = jnp.where(on[a], ref[kh, tile, node_of(a, t)], value)
                hsend[which, side, t] = value
            halo_copy(which, side).start()

    def pick(value, lane):
        return jnp.take_along_axis(value, lane, axis=1, mode="promise_in_bounds")

    def penalize(src, dst, kh, first_portion):
        def one(tile, carry):
            if kh == 0:
                pump(first_portion + tile)
            flag = flag_tab[kh]
            for a in range(4):
                lane, src_id = lane_tab[a, tile], src_tab[a, tile]
                rev, wall = rev_tab[a, tile] > 0, wall_tab[a, tile] > 0
                factor = jnp.where(wall, flag, 1.0)
                for tp in range(4):
                    ts = (tp, 7 - tp)
                    weight = edge_penalty * float(weights[tp])
                    got = [jnp.zeros((8, 128), f32) for _ in ts]
                    for b in range(4):
                        for tile_b in range(4):
                            here = src_id == 4 * b + tile_b
                            for i, t in enumerate(ts):
                                picked = pick(src[kh, tile_b, node_of(b, t)], lane)
                                got[i] = jnp.where(here, picked, got[i])
                    for i, t in enumerate(ts):
                        at = node_of(a, t)
                        other = jnp.where(rev, got[1 - i], got[i])
                        pen = weight * (factor * src[kh, tile, at] - other)
                        dst[kh, tile, at] = dst[kh, tile, at] + pen
            return carry

        lax.fori_loop(0, 4, one, 0)

    def penalize_halo(dst, kh, which):
        for side in range(2):
            halo_copy(which, side).wait_recv()

        for tile, side in ((0, 1), (3, 0)):
            for a in range(4):
                lane, here = lane_tab[a, tile], src_tab[a, tile] == 16
                rev = rev_tab[a, tile] > 0
                for tp in range(4):
                    ts = (tp, 7 - tp)
                    weight = edge_penalty * float(weights[tp])
                    got = [pick(hrecv[which, side, t], lane) for t in ts]
                    for i, t in enumerate(ts):
                        at = node_of(a, t)
                        other = jnp.where(rev, got[1 - i], got[i])
                        dst[kh, tile, at] = dst[kh, tile, at] - jnp.where(here, weight * other, 0.0)

    def part_copy(which, g):
        return pltpu.make_async_remote_copy(
            dsend.at[which], drecv.at[which, xy], ds_sem.at[which, g], dr_sem.at[which, xy],
            device_id=(g, gz), device_id_type=MESH,
        )

    def total(which):
        for d in range(1, 8):
            part_copy(which, (xy + d) % 8).start()
        drecv[which, xy] = dsend[which]

    def total_done(which, n):
        for d in range(1, 8):
            g = (xy + d) % 8
            pltpu.make_async_remote_copy(
                dsend.at[which], drecv.at[which, g], ds_sem.at[which, g],
                dr_sem.at[which, g], device_id=(g, gz), device_id_type=MESH,
            ).wait_recv()
        out = []
        for i in range(n):
            acc = drecv[which, 0, i]
            for g in range(1, 8):
                acc = acc + drecv[which, g, i]
            out.append(jnp.broadcast_to(jnp.sum(acc, axis=1, keepdims=True), (8, 128)))
        return out

    def dots(which, n, terms):
        def one(tile, accs):
            accs = list(accs)
            for i in range(64):
                for m, term in enumerate(terms(tile, i)):
                    accs[2 * m + i % 2] = accs[2 * m + i % 2] + term
            return tuple(accs)

        accs = lax.fori_loop(0, 4, one, tuple(jnp.zeros((8, 128), f32) for _ in range(2 * n)))
        for m in range(n):
            dsend[which, m] = accs[2 * m] + accs[2 * m + 1]
        total(which)

    def solve(kh):
        first_pass(kh)
        if kh == 0:
            for p in range(8, 16):
                portion(p, lambda copy: copy.start())
        send_halo(r0, kh, 2 * kh)
        penalize(r0, q1, kh, 5)
        penalize_halo(q1, kh, 2 * kh)
        send_halo(q1, kh, 2 * kh + 1)

        def terms1(tile, n):
            u, v = r0[kh, tile, n], q1[kh, tile, n]
            return u * u, u * v

        dots(2 * kh, 2, terms1)
        if kh == 0:
            pump(9)
        second_pass(kh)
        if kh == 0:
            pump(10)
        penalize(q1, q2, kh, 11)
        penalize_halo(q2, kh, 2 * kh + 1)
        rr0, pq0 = total_done(2 * kh, 2)
        alpha0 = rr0 / pq0

        def terms2(tile, n):
            u, v = r0[kh, tile, n], q1[kh, tile, n]
            r1 = u - alpha0 * v
            s = v - alpha0 * q2[kh, tile, n]
            return r1 * r1, r1 * s, r1 * v + u * s

        dots(2 * kh + 1, 3, terms2)
        if kh == 0:
            pump(15)
        return rr0, pq0

    def conclude(kh, rr0, pq0):
        def turn(tile, carry):
            for ref, out in ((r0, rt), (q1, qt)):
                rows = ref.reshape(2 * 4 * 64 * 8, 128)
                for j in range(8):
                    for k in range(8):
                        start = ((kh * 4 + tile) * 64 + 8 * j) * 8 + k
                        out[tile, k, 8 * j : 8 * j + 8, :] = rows[pl.ds(start, 8, stride=8), :]
            return carry

        lax.fori_loop(0, 4, turn, 0)
        rr1, r1s, cross = total_done(2 * kh + 1, 3)
        alpha0 = rr0 / pq0
        beta = rr1 / rr0
        alpha1 = rr1 / (r1s + beta * cross + beta * beta * pq0)
        along_r = alpha0 + alpha1 * (1.0 + beta)
        along_q = alpha1 * alpha0

        for tile in range(4):
            for k in range(8):
                out_ref[8 * kh + k, :, 128 * tile : 128 * tile + 128] = (
                    along_r[k : k + 1] * rt[tile, k] - along_q[k : k + 1] * qt[tile, k]
                )

    first_half = solve(0)
    second_half = solve(1)
    conclude(0, *first_half)
    conclude(1, *second_half)

    def sent(i, carry):
        others(i, lambda h: copy2(h, 0, 1, 12, 4).wait_send())
        return carry

    lax.fori_loop(0, 4, sent, 0)
    for p in range(16):
        portion(p, lambda copy: copy.wait_send())
    for which in range(4):
        for side in range(2):
            halo_copy(which, side).wait_send()
        for d in range(1, 8):
            part_copy(which, (xy + d) % 8).wait_send()


def per_device(concentration, geometry, nbr_elem, nbr_edge, wall_flags):
    forward, back, fourier, mass_b, weights, line = constants()
    dma = pltpu.SemaphoreType.DMA
    V = pltpu.VMEM
    i32 = jnp.int32
    anywhere = pl.BlockSpec(memory_space=pl.ANY)
    return pl.pallas_call(
        functools.partial(kernel, weights, line),
        out_shape=jax.ShapeDtypeStruct(concentration.shape, f32),
        in_specs=[anywhere] * 9,
        out_specs=pl.BlockSpec(memory_space=pltpu.VMEM),
        scratch_shapes=[
            V((2, 512), f32),
            V((4, 512), i32),
            V((4, 512), i32),
            pltpu.SMEM((16,), i32),
            V(forward.shape, bf16),
            V(back.shape, bf16),
            V(fourier.shape, bf16),
            V((64, 128), f32),
            V((4, 16, 64, 128), f32),
            V((16, 4, 64, 128), f32),
            V((16, 4, 64, 128), f32),
            V((4096, 128), f32),
            V((4096, 128), f32),
            V((16, 2, 16, 8, 128), f32),
            V((16, 2, 16, 8, 128), f32),
            V((2, 4, 64, 8, 128), f32),
            V((2, 4, 64, 8, 128), f32),
            V((2, 4, 64, 8, 128), f32),
            V((4, 8, 64, 128), f32),
            V((4, 8, 64, 128), f32),
            V((4, 4, 8, 128), i32),
            V((4, 4, 8, 128), i32),
            V((4, 4, 8, 128), i32),
            V((4, 4, 8, 128), i32),
            V((4, 4, 8, 128), i32),
            V((2, 8, 128), f32),
            V((3, 5, 8, 128), f32),
            V((2, 8, 128), f32),
            V((4, 2, 8, 8, 128), f32),
            V((4, 2, 8, 8, 128), f32),
            V((4, 3, 8, 128), f32),
            V((4, 8, 3, 8, 128), f32),
            dma((4,)),
            dma((8,)),
            dma((16,)),
            dma((16,)),
            dma((16, 6)),
            dma((16, 2)),
            dma((4, 2)),
            dma((4, 2)),
            dma((4, 8)),
            dma((4, 8)),
        ],
        compiler_params=pltpu.CompilerParams(
            collective_id=0, has_side_effects=True, vmem_limit_bytes=40 << 20
        ),
    )(
        *(
            pltpu.with_memory_space_constraint(v, pltpu.HBM)
            for v in (
                concentration, geometry, nbr_elem, nbr_edge, wall_flags,
                jnp.asarray(forward), jnp.asarray(back), jnp.asarray(fourier), jnp.asarray(mass_b),
            )
        )
    )


def solution(mesh):
    return jax.shard_map(
        per_device,
        mesh=mesh,
        in_specs=(P("gz", None, "xy"), P(None, "xy"), P(None, "xy"), P(None, "xy"), P("gz")),
        out_specs=P("gz", None, "xy"),
        check_vma=False,
    )
```

time: 128 us -> 86.8 us (0.68)
  Pallas kernels: 119 us -> 85.3 us
  local copies, waits for them, and re-layouts: 8.46 us -> 1.32 us
    pallas_call x1, Pallas kernels: 119 us -> 85.3 us  [per_device(): pl.pallas_call(functools.partial(kernel, weights, line), out_shape=jax.Sh...]
    unnamed x19 -> x1, local copies, waits for them, and re-layouts: 8.46 us -> 1.32 us
where the time goes in v1:
time: 86.8 us; the launch traced here: 86.7 us
  Pallas kernels  85.3 us (98%)
  local copies, waits for them, and re-layouts  1.32 us (2%)
    pallas_call x1, Pallas kernels, per_device(): pl.pallas_call(functools.partial(kernel, weights, line), out_shape=jax.Sh...  85.3 us

profile of v1, /device:TPU:1, one launch (start us, length us, event | category | flops | bytes accessed | tf_op | source)
XLA Modules:
  0.0 86.7 jit_solution(4732249672393966558)
XLA Ops:
  0.0 85.3 %shard_map.91 = f32[16,64,512]{2,1,0:T(8,128)S(1)} custom-call(f32[16,64,512]{2,1,0:T(8,128)} %c_ref.1, f32[2,512]{1,0:T(2,128)} %geo_hbm.1, s32[4,512]{1,0:T(4,128)} %nel_hbm.1, s32[4,512]{1,0:T(4,128)} %ned_hbm.1, s32[16]{0:T(128)} %flag_hbm.1, bf16[128,256]{1,0:T(8,128)(2,1)} %constant.8.clone.fwd_hbm, bf16[64,512]{1,0:T(8,128)(2,1)} %constant.9.clone.back_hbm, ...), custom_call_target="tpu_custom_call" | custom-call | tf_op jit(solution)/shard_map/pallas_call | solution.py:613
  85.3 1.3 %copy.11 = f32[16,64,512]{2,1,0:T(8,128)} copy(f32[16,64,512]{2,1,0:T(8,128)S(1)} %shard_map.91) | data formatting | bytes 4194304

commit v2 on v1

--- a/solution.py
+++ b/solution.py
@@ -272,8 +272,8 @@
         for pq in range(4):
             others(i, lambda h, pq=pq: copy1(h, pq).start())
 
-    issue1(0)
-    issue1(1)
+    for i in range(4):
+        issue1(i)
 
     cj, ca, cb = (coef_tab[i, 4][0:1, :] for i in range(3))
     cj4, ca4, cb4 = (jnp.concatenate([v] * 4, axis=1) for v in (cj, ca, cb))
@@ -306,12 +306,6 @@
     plane_terms(gz)
 
     def phase1(i, carry):
-        others(i, lambda h: block1(h).wait_send())
-
-        @pl.when(i < 2)
-        def _():
-            issue1(i + 2)
-
         def take(g):
             block1(g).wait_recv()
             plane_terms(g)
@@ -351,13 +345,9 @@
     lax.fori_loop(0, 8, transform, 0)
     recv2[gz] = send2[gz]
 
-    DEPTH = 3
 
     def portion(p, act):
         others(p // 4, lambda h: act(copy2(h, 1, 2 + p % 4, 4 * (p % 4), 4)))
-
-    def pump(p):
-        pass
 
     def early(i, carry):
         others(i, lambda h: copy2(h, 0, 0, 0, 12).wait_send())
@@ -397,21 +387,19 @@
             for j, value in enumerate(apply_line(line, us)):
                 dst[kh, tile, 8 * j + i] = dst[kh, tile, 8 * j + i] + cbw * value
 
-    def first_pass(kh):
+    def phase_tile(i):
+        return 2 * ((z + 1 - i // 2) % 2) + (x + 1 - i % 2) % 2
+
+    def gather_in(kh, i):
+        arrived(kh, i)
+        assemble(kh, phase_tile(i))
+
+    def loop(n, body):
         def one(i, carry):
-            arrived(kh, i)
-            if kh == 0:
-
-                @pl.when(i % 2 == 1)
-                def _():
-                    pump(3 + i // 2)
-
-            tile = 2 * ((z + 1 - i // 2) % 2) + (x + 1 - i % 2) % 2
-            assemble(kh, tile)
-            interior(r0, q1, kh, tile)
+            body(i)
             return carry
 
-        lax.fori_loop(0, 4, one, 0)
+        lax.fori_loop(0, n, one, 0)
 
     def second_pass(kh):
         def one(tile, carry):
@@ -441,10 +429,8 @@
     def pick(value, lane):
         return jnp.take_along_axis(value, lane, axis=1, mode="promise_in_bounds")
 
-    def penalize(src, dst, kh, first_portion):
+    def penalize(src, dst, kh):
         def one(tile, carry):
-            if kh == 0:
-                pump(first_portion + tile)
             flag = flag_tab[kh]
             for a in range(4):
                 lane, src_id = lane_tab[a, tile], src_tab[a, tile]
@@ -525,13 +511,8 @@
             dsend[which, m] = accs[2 * m] + accs[2 * m + 1]
         total(which)
 
-    def solve(kh):
-        first_pass(kh)
-        if kh == 0:
-            for p in range(8, 16):
-                portion(p, lambda copy: copy.start())
-        send_halo(r0, kh, 2 * kh)
-        penalize(r0, q1, kh, 5)
+    def first_matvec(kh):
+        penalize(r0, q1, kh)
         penalize_halo(q1, kh, 2 * kh)
         send_halo(q1, kh, 2 * kh + 1)
 
@@ -540,12 +521,10 @@
             return u * u, u * v
 
         dots(2 * kh, 2, terms1)
-        if kh == 0:
-            pump(9)
         second_pass(kh)
-        if kh == 0:
-            pump(10)
-        penalize(q1, q2, kh, 11)
+        penalize(q1, q2, kh)
+
+    def second_sums(kh):
         penalize_halo(q2, kh, 2 * kh + 1)
         rr0, pq0 = total_done(2 * kh, 2)
         alpha0 = rr0 / pq0
@@ -557,8 +536,6 @@
             return r1 * r1, r1 * s, r1 * v + u * s
 
         dots(2 * kh + 1, 3, terms2)
-        if kh == 0:
-            pump(15)
         return rr0, pq0
 
     def conclude(kh, rr0, pq0):
@@ -585,12 +562,29 @@
                     along_r[k : k + 1] * rt[tile, k] - along_q[k : k + 1] * qt[tile, k]
                 )
 
-    first_half = solve(0)
-    second_half = solve(1)
+    loop(4, lambda i: gather_in(0, i))
+    send_halo(r0, 0, 0)
+    for p in range(8, 16):
+        portion(p, lambda copy: copy.start())
+    loop(4, lambda tile: interior(r0, q1, 0, tile))
+    first_matvec(0)
+
+    def three(i):
+        gather_in(1, i)
+        interior(r0, q1, 1, phase_tile(i))
+
+    loop(3, three)
+    first_half = second_sums(0)
+    gather_in(1, 3)
+    send_halo(r0, 1, 2)
+    interior(r0, q1, 1, phase_tile(3))
+    first_matvec(1)
+    second_half = second_sums(1)
     conclude(0, *first_half)
     conclude(1, *second_half)
 
     def sent(i, carry):
+        others(i, lambda h: block1(h).wait_send())
         others(i, lambda h: copy2(h, 0, 1, 12, 4).wait_send())
         return carry
 

time: 86.8 us -> 84.9 us (0.978)
  Pallas kernels: 85.3 us -> 83.4 us
    pallas_call x1, Pallas kernels: 85.3 us -> 83.4 us  [per_device(): pl.pallas_call(functools.partial(kernel, weights, line), out_shape=jax.Sh...]
where the time goes in v2:
time: 84.9 us; the launch traced here: 84.8 us
  Pallas kernels  83.4 us (98%)
  local copies, waits for them, and re-layouts  1.32 us (2%)
    pallas_call x1, Pallas kernels, per_device(): pl.pallas_call(functools.partial(kernel, weights, line), out_shape=jax.Sh...  83.4 us

profile of v2, /device:TPU:1, one launch (start us, length us, event | category | flops | bytes accessed | tf_op | source)
XLA Modules:
  0.0 84.8 jit_solution(17094837129397137395)
XLA Ops:
  0.0 83.4 %shard_map.91 = f32[16,64,512]{2,1,0:T(8,128)S(1)} custom-call(f32[16,64,512]{2,1,0:T(8,128)} %c_ref.1, f32[2,512]{1,0:T(2,128)} %geo_hbm.1, s32[4,512]{1,0:T(4,128)} %nel_hbm.1, s32[4,512]{1,0:T(4,128)} %ned_hbm.1, s32[16]{0:T(128)} %flag_hbm.1, bf16[128,256]{1,0:T(8,128)(2,1)} %constant.8.clone.fwd_hbm, bf16[64,512]{1,0:T(8,128)(2,1)} %constant.9.clone.back_hbm, ...), custom_call_target="tpu_custom_call" | custom-call | tf_op jit(solution)/shard_map/pallas_call | solution.py:607
  83.4 1.3 %copy.11 = f32[16,64,512]{2,1,0:T(8,128)} copy(f32[16,64,512]{2,1,0:T(8,128)S(1)} %shard_map.91) | data formatting | bytes 4194304

commit v3 on v2

--- a/solution.py
+++ b/solution.py
@@ -305,15 +305,19 @@
 
     plane_terms(gz)
 
+    def take(*places):
+        for p in places:
+            block1(source(p)).wait_recv()
+        for p in places:
+            plane_terms(source(p))
+
     def phase1(i, carry):
-        def take(g):
-            block1(g).wait_recv()
-            plane_terms(g)
-
-        others(i, take)
+        take(2 * i, 2 * i + 1)
         return carry
 
-    lax.fori_loop(0, 4, phase1, 0)
+    lax.fori_loop(0, 6, phase1, 0)
+    take(13)
+    take(14, 15)
 
     def copy2(h, kh, which, start, size):
         rows = pl.ds(start, size)
@@ -490,12 +494,14 @@
                 dsend.at[which], drecv.at[which, g], ds_sem.at[which, g],
                 dr_sem.at[which, g], device_id=(g, gz), device_id_type=MESH,
             ).wait_recv()
+        acc = drecv[which, 0]
+        for g in range(1, 8):
+            acc = acc + drecv[which, g]
+        group = lane_groups((8, 128))
         out = []
-        for i in range(n):
-            acc = drecv[which, 0, i]
-            for g in range(1, 8):
-                acc = acc + drecv[which, g, i]
-            out.append(jnp.broadcast_to(jnp.sum(acc, axis=1, keepdims=True), (8, 128)))
+        for m in range(n):
+            mine = jnp.sum(jnp.where(group == m, acc, 0.0), axis=1, keepdims=True)
+            out.append(jnp.broadcast_to(mine, (8, 128)))
         return out
 
     def dots(which, n, terms):
@@ -507,8 +513,14 @@
             return tuple(accs)
 
         accs = lax.fori_loop(0, 4, one, tuple(jnp.zeros((8, 128), f32) for _ in range(2 * n)))
+        group = lane_groups((8, 128))
+        packed = jnp.zeros((8, 128), f32)
         for m in range(n):
-            dsend[which, m] = accs[2 * m] + accs[2 * m + 1]
+            folded = accs[2 * m] + accs[2 * m + 1]
+            folded = folded + pltpu.roll(folded, 64, 1)
+            folded = folded + pltpu.roll(folded, 32, 1)
+            packed = jnp.where(group == m, folded, packed)
+        dsend[which] = packed
         total(which)
 
     def first_matvec(kh):
@@ -640,8 +652,8 @@
             V((2, 8, 128), f32),
             V((4, 2, 8, 8, 128), f32),
             V((4, 2, 8, 8, 128), f32),
-            V((4, 3, 8, 128), f32),
-            V((4, 8, 3, 8, 128), f32),
+            V((4, 8, 128), f32),
+            V((4, 8, 8, 128), f32),
             dma((4,)),
             dma((8,)),
             dma((16,)),

time: 84.9 us -> 84.3 us (level)
  no operation moved by 1% of the time
where the time goes in v3:
time: 84.3 us; the launch traced here: 84.1 us
  Pallas kernels  82.8 us (98%)
  local copies, waits for them, and re-layouts  1.32 us (2%)
    pallas_call x1, Pallas kernels, per_device(): pl.pallas_call(functools.partial(kernel, weights, line), out_shape=jax.Sh...  82.8 us

profile of v3, /device:TPU:1, one launch (start us, length us, event | category | flops | bytes accessed | tf_op | source)
XLA Modules:
  0.0 84.1 jit_solution(9026184264044351048)
XLA Ops:
  0.0 82.8 %shard_map.91 = f32[16,64,512]{2,1,0:T(8,128)S(1)} custom-call(f32[16,64,512]{2,1,0:T(8,128)} %c_ref.1, f32[2,512]{1,0:T(2,128)} %geo_hbm.1, s32[4,512]{1,0:T(4,128)} %nel_hbm.1, s32[4,512]{1,0:T(4,128)} %ned_hbm.1, s32[16]{0:T(128)} %flag_hbm.1, bf16[128,256]{1,0:T(8,128)(2,1)} %constant.8.clone.fwd_hbm, bf16[64,512]{1,0:T(8,128)(2,1)} %constant.9.clone.back_hbm, ...), custom_call_target="tpu_custom_call" | custom-call | tf_op jit(solution)/shard_map/pallas_call | solution.py:619
  82.8 1.3 %copy.11 = f32[16,64,512]{2,1,0:T(8,128)} copy(f32[16,64,512]{2,1,0:T(8,128)S(1)} %shard_map.91) | data formatting | bytes 4194304
